TPU v7x, 32 devices: a whole 2x2x4 slice. The times are simulated.
32 devices in a mesh: groups: 2 (over x), leaf: 16 (over z, y, core).
Axes of the slice: x: 2, y: 2, z: 4, core: 2. Of those that a mesh axis runs over, the one named last changes fastest.
Arguments:
- right_side: float32 [65536, 256], P(('groups', 'leaf')), parts along dimension 0, may hold values from -6 to 6
- cotangent: float32 [65536, 256], P(('groups', 'leaf')), parts along dimension 0, may hold values from -6 to 6
- coeff_basis: float32 [4, 64, 65536], P(None, None, ('groups', 'leaf')), parts along dimension 2, may hold values from -1 to 1
- saved_basis: float32 [4, 64, 65536], P(None, None, ('groups', 'leaf')), parts along dimension 2, may hold values from -0.24 to 0.24
- node_inverse: float32 [30, 128, 128], P('groups'), parts along dimension 0, may hold values from -1 to 2.5
- leaf_rows: int32 [32], P(('groups', 'leaf')), parts along dimension 0, may hold values from 1 to 2048, 24576 in all
Outputs:
- solution: float32 [65536, 256], P(('groups', 'leaf')), parts along dimension 0
- grad_left: bfloat16 [4, 64, 65536], P(None, None, ('groups', 'leaf')), parts along dimension 2
- grad_right: bfloat16 [4, 64, 65536], P(None, None, ('groups', 'leaf')), parts along dimension 2
There are 2 independent parts, one for each index of `groups`. A program takes and returns all parts, laid end to end along the dimension named above; each array names one. Nothing has to cross between parts.
Inputs may be any that keep to these rules, and one draw needn't show every extreme that they name: `leaf_rows`: every leaf has at least one live row; the live rows of all leaves sum to 24576, and some leaf has all 2048 rows live.
All inputs are finite; a program needn't handle non-finite values. No bound on the sum of `leaf_rows` on one device may be relied on, other than what follows from the above.
Results may differ from a plain program's by a relative error of at most 0.001.
Values sent between devices are 32-bit elements; how exact they have to be, the bound alone decides.
A program may use at most 64 MiB of HBM per device.

v0:
```python
import jax
import jax.numpy as jnp
from jax import lax
from jax.sharding import PartitionSpec as P

HI = lax.Precision.HIGHEST
MID = lax.Precision.HIGH


def swapped(value, bit):
    mask = 2**bit
    pairs = [(source, source ^ mask) for source in range(lax.axis_size("leaf"))]
    return lax.ppermute(value, "leaf", pairs)


def dot(a, b, dims=((1,), (0,)), precision=MID):
    return lax.dot_general(
        a, b, (dims, ((), ())), precision=precision, preferred_element_type=jnp.float32
    )


def tree(sums, weight_sums, gram, node_inverse, levels, rank, base):
    position = lax.axis_index("leaf")
    cols = sums.shape[1]
    half = cols // 2
    mine = jnp.right_shift(position, base) % 2
    s_own = lax.dynamic_slice_in_dim(sums, mine * half, half, 1)
    s_other = lax.dynamic_slice_in_dim(sums, (1 - mine) * half, half, 1)
    k_own = lax.dynamic_slice_in_dim(weight_sums, mine * half, half, 1)
    k_other = lax.dynamic_slice_in_dim(weight_sums, (1 - mine) * half, half, 1)
    g_own = gram
    z_list, c_list, k_list, row_list = [], [], [], []
    c_first, k_first, row_first = s_own[:rank], k_own[:rank], g_own[:rank]
    for height in range(levels):
        if height == 0:
            sent = jnp.concatenate([s_other, k_other, g_own], 1)
        else:
            sent = jnp.concatenate([s_own, k_own, g_own], 1)
        got = swapped(sent, base + height)
        s_sib, k_sib, g_sib = got[:, :half], got[:, half : 2 * half], got[:, 2 * half :]
        place = jnp.right_shift(position, base + height) % 2
        offset = 2**levels - 2 ** (levels - height)
        inverse = lax.dynamic_index_in_dim(
            node_inverse, offset + jnp.right_shift(position, base + height + 1), 0, keepdims=False
        )
        inverse = jnp.where(place == 0, inverse, jnp.roll(inverse, (rank, rank), (0, 1)))
        pair = jnp.concatenate([s_own[:rank], s_sib[:rank]], 0)
        z = dot(inverse, pair, precision=HI)
        z_list.append(z)
        c_list.append(s_sib[:rank])
        k_list.append(k_sib[:rank])
        row_list.append(g_sib[:rank])
        if height < levels - 1:
            response = jnp.concatenate([g_own[rank:, :rank], g_sib[rank:, :rank]], 1)
            s_own = s_own[rank:] + s_sib[rank:] - dot(response, z, precision=HI)
            k_own = k_own[rank:] + k_sib[rank:]
            g_own = (g_own + g_sib)[rank:, rank:]
    l_list = []
    for height in range(levels):
        z_chain = jnp.concatenate(
            [z_list[height][rank:]] + [z[:rank] for z in z_list[height + 1 :]], 0
        )
        l_list.append(c_list[height] - dot(row_list[height], z_chain, precision=HI))
    scale = 1.0 / jnp.sqrt(jnp.float32(cols))
    z_own = jnp.concatenate([z[:rank] for z in z_list], 0)
    l_first = c_first - dot(row_first, z_own, precision=HI)

    def pack(z_first, l_zero, k_zero):
        return jnp.concatenate(
            [z_first, z_own[rank:], l_zero * scale]
            + [l * scale for l in l_list[1:]]
            + [k_zero * scale]
            + [k * scale for k in k_list[1:]],
            0,
        )

    packed = pack(z_own[:rank], l_list[0], k_list[0])
    other = swapped(pack(z_list[0][rank:], l_first, k_first), base)
    full = jnp.where(
        mine == 0,
        jnp.concatenate([packed, other], 1),
        jnp.concatenate([other, packed], 1),
    )
    rows = levels * rank
    return full[:rows], full[rows : 2 * rows], full[2 * rows :]


def body(right_side, cotangent, coeff_basis, saved_basis, node_inverse, leaf_rows):
    row_count = right_side.shape[0]
    levels, rank = coeff_basis.shape[0], coeff_basis.shape[1]
    base = lax.axis_size("leaf").bit_length() - 1 - levels
    live = (jnp.arange(row_count, dtype=jnp.int32) < leaf_rows[0]).astype(jnp.float32)
    basis = coeff_basis.reshape(levels * rank, row_count) * live[None, :]
    saved = saved_basis.reshape(levels * rank, row_count)
    sums = dot(basis, right_side)
    weight_sums = dot(basis, cotangent)
    gram = dot(basis, saved, ((1,), (1,)))
    for bit in range(base):
        sums = sums + swapped(sums, bit)
        weight_sums = weight_sums + swapped(weight_sums, bit)
        gram = gram + swapped(gram, bit)
    z_own, l_sib, k_sib = tree(sums, weight_sums, gram, node_inverse, levels, rank, base)
    current = (right_side - dot(saved, z_own, ((0,), (0,)))) * live[:, None]
    left = dot(l_sib, cotangent, ((1,), (1,))) * live[None, :]
    right = dot(k_sib, current, ((1,), (1,)))
    shape = (levels, rank, row_count)
    return (
        current,
        left.astype(jnp.bfloat16).reshape(shape),
        right.astype(jnp.bfloat16).reshape(shape),
    )


def solution(mesh):
    in_specs = (
        P(("groups", "leaf"), None),
        P(("groups", "leaf"), None),
        P(None, None, ("groups", "leaf")),
        P(None, None, ("groups", "leaf")),
        P("groups", None, None),
        P(("groups", "leaf")),
    )
    out_specs = (
        P(("groups", "leaf"), None),
        P(None, None, ("groups", "leaf")),
        P(None, None, ("groups", "leaf")),
    )
    return jax.shard_map(body, mesh=mesh, in_specs=in_specs, out_specs=out_specs, check_vma=False)
```

profile of v0, /device:TPU:0, one launch (start us, length us, event | category | flops | bytes accessed | tf_op | source)
XLA Modules:
  0.0 87.1 jit_solution(11828385242695079519)
XLA Ops:
  1.5 3.4 %bitcast_multiply_fusion = f32[256,2048]{1,0:T(8,128)} fusion(f32[4,64,2048]{2,1,0:T(8,128)} %param.8, f32[2048]{0:T(1024)S(1)} %fusion.98), kind=kLoop, calls=%fused_computation.6 | loop fusion | flops 524288 | bytes 4202496 | tf_op jit(solution)/shard_map/mul | solution.py:93
  4.9 1.6 %broadcast_multiply_fusion = f32[4,64,2048]{2,1,0:T(8,128)} fusion(f32[4,64,2048]{2,1,0:T(8,128)S(1)} %copy-done.3, f32[2048]{0:T(1024)S(1)} %fusion.98), kind=kLoop, calls=%fused_computation.19 | loop fusion | flops 524288 | bytes 4202496 | tf_op jit(solution)/shard_map/mul | solution.py:93
  6.4 3.4 %fusion.115 = f32[256,256]{1,0:T(8,128)S(1)} fusion(f32[256,2048]{1,0:T(8,128)} %bitcast_multiply_fusion, f32[2048,256]{1,0:T(8,128)} %param.6), kind=kOutput, calls=%fused_computation.182 | convolution fusion | flops 805306368 | bytes 4456448 | tf_op jit(solution)/shard_map/dot_general | solution.py:17
  9.9 1.1 %fusion.116 = f32[256,256]{1,0:T(8,128)S(1)} fusion(f32[256,2048]{1,0:T(8,128)S(1)} %copy-done.1, f32[2048,256]{1,0:T(8,128)S(1)} %copy-done.4), kind=kOutput, calls=%fused_computation.183 | convolution fusion | flops 805306368 | bytes 4456448 | tf_op jit(solution)/shard_map/dot_general | solution.py:17
  11.1 2.6 %fusion.117 = f32[256,256]{1,0:T(8,128)S(1)} fusion(f32[256,2048]{1,0:T(8,128)} %bitcast.64, f32[256,2048]{1,0:T(8,128)S(1)} %bitcast.62), kind=kOutput, calls=%fused_computation.184 | convolution fusion | flops 805306368 | bytes 4456448 | tf_op jit(solution)/shard_map/dot_general | solution.py:17
  15.1 1.5 %dynamic-slice_bitcast_fusion.1 = (f32[64,128]{1,0:T(8,128)S(1)}, f32[64,128]{1,0:T(8,128)}, f32[64,128]{1,0:T(8,128)S(1)}, f32[64,128]{1,0:T(8,128)S(1)}, f32[6...) fusion(f32[15,128,128]{2,1,0:T(8,128)} %param.10, s32[]{:T(128)S(6)} %select_n.93, ...), kind=kLoop, calls=%fused_computation.146 | loop fusion | bytes 524308 | tf_op jit(solution)/shard_map/jit(_roll_static)/slice | solution.py:46
  17.5 1.0 %slice_add_fusion = f32[256,256]{1,0:T(8,128)S(1)} fusion(f32[256,256]{1,0:T(8,128)S(1)} %fusion.117, f32[256,512]{1,0:T(8,128)} %collective-permute-done), kind=kLoop, calls=%fused_computation.26 | loop fusion | flops 65536 | bytes 786432 | tf_op jit(solution)/shard_map/add | solution.py:57
  19.3 1.1 %fusion.48 = f32[128,128]{1,0:T(8,128)S(1)} fusion(f32[64,128]{1,0:T(8,128)S(1)} %get-tuple-element.12, f32[64,128]{1,0:T(8,128)S(1)} %get-tuple-element.13, f32[128,64]{1,0:T(8,128)S(1)} %slice_maximum_fusion.3, f32[64,128]{1,0:T(8,128)S(1)} %slice.350, f32[64,128]{1,0:T(8,128)S(1)} %constant_dynamic-slice_fusion, f32[15,128,128]{2,1,0:T(8,128)} %param.10, ...), kind=kOutput, calls=%fused_computation.77 | convolution fusion | flops 25231360 | bytes 294917 | tf_op jit(solution)/shard_map/dot_general | solution.py:17
  21.4 0.9 %slice_add_fusion.2 = f32[192,128]{1,0:T(8,128)S(1)} fusion(f32[256,512]{1,0:T(8,128)} %collective-permute-done, f32[256,256]{1,0:T(8,128)S(1)} %fusion.116, s32[]{:T(128)S(6)} %add.87, s32[]{:T(128)S(6)} %select_n.81), kind=kLoop, calls=%fused_computation.37 | loop fusion | flops 24576 | bytes 294920 | tf_op jit(solution)/shard_map/add | solution.py:56
  22.3 1.2 %fusion.15 = f32[192,128]{1,0:T(8,128)S(1)} fusion(f32[256,512]{1,0:T(8,128)} %collective-permute-done, f32[256,256]{1,0:T(8,128)S(1)} %fusion.115, s32[]{:T(128)S(6)} %add.87, s32[]{:T(128)S(6)} %select_n.81, f32[128,128]{1,0:T(8,128)S(1)} %fusion.48, f32[192,64]{1,0:T(8,128)S(1)} %slice.356, f32[192,64]{1,0:T(8,128)S(1)} %slice.355), kind=kOutput, calls=%fused_computation.39 | convolution fusion | flops 37822464 | bytes 458760 | tf_op jit(solution)/shard_map/dot_general | solution.py:17
  24.3 2.5 %collective-permute-start.1 = (f32[192,448]{1,0:T(8,128)}, f32[192,448]{1,0:T(8,128)}, u32[]{:S(2)}, u32[]{:S(2)}) collective-permute-start(f32[192,448]{1,0:T(8,128)} %pad_maximum_fusion.1), channel_id=1, source_target_pairs={{0,2},{1,3},{2,0},{3,1},{4,6},{5,7},{6,4},{7,5},{8,10},{9,11},{10,... | collective-permute-start | bytes 1032200 | tf_op jit(solution)/shard_map/ppermute | solution.py:13
  28.5 8.4 %collective-permute-done.1 = f32[192,448]{1,0:T(8,128)} collective-permute-done((f32[192,448]{1,0:T(8,128)}, f32[192,448]{1,0:T(8,128)}, u32[]{:S(2)}, u32[]{:S(2)}) %collective-permute-start.1) | collective-permute-done | bytes 344096 | tf_op jit(solution)/shard_map/ppermute | solution.py:13
  36.9 1.0 %slice_add_fusion.1 = f32[192,192]{1,0:T(8,128)S(1)} fusion(f32[192,448]{1,0:T(8,128)} %collective-permute-done.1, f32[256,256]{1,0:T(8,128)S(1)} %slice_add_fusion), kind=kLoop, calls=%fused_computation.27 | loop fusion | flops 36864 | bytes 442368 | tf_op jit(solution)/shard_map/add | solution.py:57
  38.8 1.2 %fusion.43 = f32[128,128]{1,0:T(8,128)S(1)} fusion(f32[64,128]{1,0:T(8,128)} %copy-done.10, f32[64,128]{1,0:T(8,128)} %copy-done.11, f32[128,64]{1,0:T(8,128)} %slice_maximum_fusion.2, f32[64,128]{1,0:T(8,128)S(1)} %slice.361, f32[64,128]{1,0:T(8,128)S(1)} %slice.357, f32[15,128,128]{2,1,0:T(8,128)} %param.10, s32[]{:T(128)S(6)} %select_n.85, pred[]{:T(512)S(6)} %eq.20), kind=kOutput, calls=%fused_computation.71 | convolution fusion | flops 25231360 | bytes 327685 | tf_op jit(solution)/shard_map/dot_general | solution.py:17
  40.9 1.1 %fusion.35 = f32[128,128]{1,0:T(8,128)S(1)} fusion(f32[192,448]{1,0:T(8,128)} %collective-permute-done.1, f32[192,128]{1,0:T(8,128)S(1)} %fusion.15, f32[128,128]{1,0:T(8,128)S(1)} %fusion.43, f32[128,64]{1,0:T(8,128)S(1)} %slice.368, f32[128,64]{1,0:T(8,128)S(1)} %slice.367), kind=kOutput, calls=%fused_computation.61 | convolution fusion | flops 25214976 | bytes 327680 | tf_op jit(solution)/shard_map/dot_general | solution.py:17
  42.9 1.9 %collective-permute-start.2 = (f32[128,384]{1,0:T(8,128)S(1)}, f32[128,384]{1,0:T(8,128)S(1)}, u32[]{:S(2)}, u32[]{:S(2)}) collective-permute-start(f32[128,384]{1,0:T(8,128)S(1)} %pad_maximum_fusion.2), channel_id=1, source_target_pairs={{0,4},{1,5},{2,6},{3,7},{4,0},{5,1},{6,2},{7,3},{8,12},{9,13},{10,... | collective-permute-start | bytes 589832 | tf_op jit(solution)/shard_map/ppermute | solution.py:13
  45.4 4.3 %collective-permute-done.2 = f32[128,384]{1,0:T(8,128)S(1)} collective-permute-done((f32[128,384]{1,0:T(8,128)S(1)}, f32[128,384]{1,0:T(8,128)S(1)}, u32[]{:S(2)}, u32[]{:S(2)}) %collective-permute-start.2) | collective-permute-done | bytes 196640 | tf_op jit(solution)/shard_map/ppermute | solution.py:13
  49.8 1.1 %fusion.38 = f32[128,128]{1,0:T(8,128)S(1)} fusion(f32[64,128]{1,0:T(8,128)S(1)} %copy-done.7, f32[64,128]{1,0:T(8,128)S(1)} %copy-done.9, f32[128,64]{1,0:T(8,128)S(1)} %slice_maximum_fusion.1, f32[64,128]{1,0:T(8,128)S(1)} %get-tuple-element.19, f32[64,128]{1,0:T(8,128)S(1)} %slice.369, f32[15,128,128]{2,1,0:T(8,128)} %param.10, s32[]{:T(128)S(6)} %select_n.89, ...), kind=kOutput, calls=%fused_computation.65 | convolution fusion | flops 25231360 | bytes 294917 | tf_op jit(solution)/shard_map/dot_general | solution.py:17
  51.2 2.6 %collective-permute-start.3 = (f32[64,320]{1,0:T(8,128)S(1)}, f32[64,320]{1,0:T(8,128)S(1)}, u32[]{:S(2)}, u32[]{:S(2)}) collective-permute-start(f32[64,320]{1,0:T(8,128)S(1)} %pad_maximum_fusion.11), channel_id=1, source_target_pairs={{0,8},{1,9},{2,10},{3,11},{4,12},{5,13},{6,14},{7,15},{8,0},{9,1},... | collective-permute-start | bytes 245768 | tf_op jit(solution)/shard_map/ppermute | solution.py:13
  54.4 3.6 %collective-permute-done.3 = f32[64,320]{1,0:T(8,128)S(1)} collective-permute-done((f32[64,320]{1,0:T(8,128)S(1)}, f32[64,320]{1,0:T(8,128)S(1)}, u32[]{:S(2)}, u32[]{:S(2)}) %collective-permute-start.3) | collective-permute-done | bytes 81952 | tf_op jit(solution)/shard_map/ppermute | solution.py:13
  58.0 1.1 %fusion.32 = f32[128,128]{1,0:T(8,128)S(1)} fusion(f32[64,128]{1,0:T(8,128)S(1)} %copy-done.5, f32[64,128]{1,0:T(8,128)S(1)} %get-tuple-element.6, f32[128,64]{1,0:T(8,128)S(1)} %slice_maximum_fusion, f32[64,128]{1,0:T(8,128)S(1)} %slice.387, f32[64,128]{1,0:T(8,128)S(1)} %fusion.87, f32[15,128,128]{2,1,0:T(8,128)} %param.10, s32[]{:T(128)S(6)} %select_n.93, ...), kind=kOutput, calls=%fused_computation.56 | convolution fusion | flops 25231360 | bytes 294917 | tf_op jit(solution)/shard_map/dot_general | solution.py:17
  60.6 1.7 %fusion.9 = f32[768,128]{1,0:T(8,128)} fusion(f32[768,128]{1,0:T(8,128)} %get-tuple-element.26, f32[64,128]{1,0:T(8,128)S(1)} %get-tuple-element.28, f32[64,128]{1,0:T(8,128)S(1)} %get-tuple-element.32, f32[64,128]{1,0:T(8,128)S(1)} %get-tuple-element.36, f32[64,128]{1,0:T(8,128)S(1)} %get-tuple-element.22, f32[256,512]{1,0:T(8,128)} %collective-permute-done), kind=kOutput, calls=%fused_computation.18 | convolution fusion | flops 25280512 | bytes 262144 | tf_op jit(solution)/shard_map/dot_general | solution.py:17
  62.3 1.7 %constant_dynamic-update-slice_fusion.6 = (f32[768,128]{1,0:T(8,128)}, f32[768,128]{1,0:T(8,128)}) fusion(f32[768,128]{1,0:T(8,128)} %fusion.9, f32[768,128]{1,0:T(8,128)} %fusion.4, f32[64,128]{1,0:T(8,128)S(1)} %get-tuple-element.28, f32[64,128]{1,0:T(8,128)S(1)} %get-tuple-element.32, f32[64,128]{1,0:T(8,128)S(1)} %get-tuple-element.35, ...), kind=kOutput, calls=%fused_computation.117 | convolution fusion | flops 18939904 | bytes 262144 | tf_op jit(solution)/shard_map/dot_general | solution.py:17
  66.2 1.4 %constant_dynamic-update-slice_fusion.3 = f32[768,128]{1,0:T(8,128)} fusion(f32[768,128]{1,0:T(8,128)} %get-tuple-element.37, f32[256,512]{1,0:T(8,128)} %collective-permute-done), kind=kLoop, calls=%fused_computation.114 | loop fusion | flops 8192 | bytes 65536
  67.6 1.4 %constant_dynamic-update-slice_fusion.2 = (f32[768,128]{1,0:T(8,128)}, f32[768,128]{1,0:T(8,128)}) fusion(f32[768,128]{1,0:T(8,128)} %constant_dynamic-update-slice_fusion.3, f32[192,448]{1,0:T(8,128)} %collective-permute-done.1, f32[768,128]{1,0:T(8,128)} %constant_dynamic-update-slice_fusion.14), kind=kLoop, calls=%fused_computation.113 | loop fusion | flops 8192 | bytes 98304
  70.2 2.9 %copy.9 = f32[2048,256]{0,1:T(8,128)} copy(f32[2048,256]{1,0:T(8,128)} %param.6) | data formatting | bytes 4194304 | tf_op args[0]
  73.1 1.2 %maximum_select_fusion = f32[768,256]{1,0:T(8,128)S(1)} fusion(f32[768,128]{1,0:T(8,128)S(1)} %collective-permute-done.4, f32[768,128]{1,0:T(8,128)} %get-tuple-element.20, pred[]{:T(512)S(6)} %eq.19), kind=kLoop, calls=%fused_computation.20 | loop fusion | flops 589824 | bytes 1572865 | tf_op jit(solution)/shard_map/jit(_where)/select_n | solution.py:79
  74.3 2.8 %fusion.1 = f32[2048,256]{0,1:T(8,128)S(1)} fusion(f32[2048,256]{0,1:T(8,128)} %copy.9, f32[256,2048]{1,0:T(8,128)S(1)} %bitcast.63, f32[2048]{0:T(1024)S(1)} %fusion.98, f32[768,256]{1,0:T(8,128)S(1)} %maximum_select_fusion), kind=kOutput, calls=%fused_computation.3 | convolution fusion | flops 806354944 | bytes 6561792 | tf_op jit(solution)/shard_map/dot_general | solution.py:17
  77.1 1.3 %copy-done.2 = f32[2048,256]{0,1:T(8,128)} copy-done((f32[2048,256]{0,1:T(8,128)}, f32[2048,256]{0,1:T(8,128)S(1)}, u32[]{:S(2)}) %copy-start.2) | copy-done | bytes 2097176
  78.5 2.2 %convolution_convert_fusion = bf16[256,2048]{1,0:T(8,128)(2,1)} fusion(f32[2048,256]{0,1:T(8,128)S(1)} %fusion.1, f32[768,256]{1,0:T(8,128)S(1)} %maximum_select_fusion), kind=kOutput, calls=%fused_computation.5 | convolution fusion | flops 805830656 | bytes 3407872 | tf_op jit(solution)/shard_map/dot_general | solution.py:17
  80.6 2.9 %copy.10 = f32[2048,256]{1,0:T(8,128)} copy(f32[2048,256]{0,1:T(8,128)} %copy-done.2) | data formatting | bytes 4194304
  83.5 3.6 %fusion.2 = bf16[256,2048]{1,0:T(8,128)(2,1)} fusion(f32[2048,256]{1,0:T(8,128)} %param.7, f32[2048]{0:T(1024)S(1)} %fusion.98, f32[768,256]{1,0:T(8,128)S(1)} %maximum_select_fusion), kind=kOutput, calls=%fused_computation.4 | convolution fusion | flops 806354944 | bytes 3416064 | tf_op jit(solution)/shard_map/dot_general | solution.py:17
  (70 shorter events, 15.7 us)
Async XLA Ops:
  0.6 10.4 %copy-start = (f32[4,64,2048]{2,1,0:T(8,128)S(1)}, f32[4,64,2048]{2,1,0:T(8,128)}, u32[]{:S(2)}) copy-start(f32[4,64,2048]{2,1,0:T(8,128)} %param.9) | copy-start | bytes 6291460
  1.5 3.4 %copy-start.3 = (f32[4,64,2048]{2,1,0:T(8,128)S(1)}, f32[4,64,2048]{2,1,0:T(8,128)}, u32[]{:S(2)}) copy-start(f32[4,64,2048]{2,1,0:T(8,128)} %param.8) | copy-start | bytes 6291460
  6.4 3.4 %copy-start.1 = (f32[256,2048]{1,0:T(8,128)S(1)}, f32[256,2048]{1,0:T(8,128)}, u32[]{:S(2)}) copy-start(f32[256,2048]{1,0:T(8,128)} %bitcast_multiply_fusion) | copy-start | bytes 6291460
  6.4 3.5 %copy-start.4 = (f32[2048,256]{1,0:T(8,128)S(1)}, f32[2048,256]{1,0:T(8,128)}, u32[]{:S(2)}) copy-start(f32[2048,256]{1,0:T(8,128)} %param.7) | copy-start | bytes 6291460
  14.6 2.9 %collective-permute-start = (f32[256,512]{1,0:T(8,128)}, f32[256,512]{1,0:T(8,128)}, u32[]{:S(2)}, u32[]{:S(2)}) collective-permute-start(f32[256,512]{1,0:T(8,128)} %pad_maximum_fusion), channel_id=1, source_target_pairs={{0,1},{1,0},{2,3},{3,2},{4,5},{5,4},{6,7},{7,6},{8,9},{9,8},{10,11... | collective-permute-start | bytes 1572872 | tf_op jit(solution)/shard_map/ppermute | solution.py:13
  15.1 5.3 %copy-start.12 = (f32[64,128]{1,0:T(8,128)}, f32[64,128]{1,0:T(8,128)S(1)}, u32[]{:S(2)}) copy-start(f32[64,128]{1,0:T(8,128)S(1)} %constant_dynamic-slice_fusion) | copy-start | bytes 98308
  16.7 0.8 copy-start.10
  16.7 0.8 copy-start.11
  16.7 10.1 %copy-start.6 = (f32[64,128]{1,0:T(8,128)}, f32[64,128]{1,0:T(8,128)S(1)}, u32[]{:S(2)}) copy-start(f32[64,128]{1,0:T(8,128)S(1)} %get-tuple-element.8) | copy-start | bytes 98308
  16.7 10.1 %copy-start.8 = (f32[64,128]{1,0:T(8,128)}, f32[64,128]{1,0:T(8,128)S(1)}, u32[]{:S(2)}) copy-start(f32[64,128]{1,0:T(8,128)S(1)} %get-tuple-element.9) | copy-start | bytes 98308
  24.3 12.6 %collective-permute-start.1 = (f32[192,448]{1,0:T(8,128)}, f32[192,448]{1,0:T(8,128)}, u32[]{:S(2)}, u32[]{:S(2)}) collective-permute-start(f32[192,448]{1,0:T(8,128)} %pad_maximum_fusion.1), channel_id=1, source_target_pairs={{0,2},{1,3},{2,0},{3,1},{4,6},{5,7},{6,4},{7,5},{8,10},{9,11},{10,... | collective-permute-start | bytes 1032200 | tf_op jit(solution)/shard_map/ppermute | solution.py:13
  26.9 22.9 %copy-start.7 = (f32[64,128]{1,0:T(8,128)S(1)}, f32[64,128]{1,0:T(8,128)}, u32[]{:S(2)}) copy-start(f32[64,128]{1,0:T(8,128)} %copy-done.6) | copy-start | bytes 98308
  26.9 22.9 %copy-start.9 = (f32[64,128]{1,0:T(8,128)S(1)}, f32[64,128]{1,0:T(8,128)}, u32[]{:S(2)}) copy-start(f32[64,128]{1,0:T(8,128)} %copy-done.8) | copy-start | bytes 98308
  27.8 30.2 %copy-start.5 = (f32[64,128]{1,0:T(8,128)S(1)}, f32[64,128]{1,0:T(8,128)}, u32[]{:S(2)}) copy-start(f32[64,128]{1,0:T(8,128)} %get-tuple-element.7) | copy-start | bytes 98308
  37.9 21.8 %copy-start.13 = (f32[64,128]{1,0:T(8,128)S(1)}, f32[64,128]{1,0:T(8,128)}, u32[]{:S(2)}) copy-start(f32[64,128]{1,0:T(8,128)} %copy-done.12) | copy-start | bytes 98308
  42.9 6.8 %collective-permute-start.2 = (f32[128,384]{1,0:T(8,128)S(1)}, f32[128,384]{1,0:T(8,128)S(1)}, u32[]{:S(2)}, u32[]{:S(2)}) collective-permute-start(f32[128,384]{1,0:T(8,128)S(1)} %pad_maximum_fusion.2), channel_id=1, source_target_pairs={{0,4},{1,5},{2,6},{3,7},{4,0},{5,1},{6,2},{7,3},{8,12},{9,13},{10,... | collective-permute-start | bytes 589832 | tf_op jit(solution)/shard_map/ppermute | solution.py:13
  51.2 6.8 %collective-permute-start.3 = (f32[64,320]{1,0:T(8,128)S(1)}, f32[64,320]{1,0:T(8,128)S(1)}, u32[]{:S(2)}, u32[]{:S(2)}) collective-permute-start(f32[64,320]{1,0:T(8,128)S(1)} %pad_maximum_fusion.11), channel_id=1, source_target_pairs={{0,8},{1,9},{2,10},{3,11},{4,12},{5,13},{6,14},{7,15},{8,0},{9,1},... | collective-permute-start | bytes 245768 | tf_op jit(solution)/shard_map/ppermute | solution.py:13
  70.2 2.9 %collective-permute-start.4 = (f32[768,128]{1,0:T(8,128)}, f32[768,128]{1,0:T(8,128)S(1)}, u32[]{:S(2)}, u32[]{:S(2)}) collective-permute-start(f32[768,128]{1,0:T(8,128)} %get-tuple-element.21), channel_id=1, source_target_pairs={{0,1},{1,0},{2,3},{3,2},{4,5},{5,4},{6,7},{7,6},{8,9},{9,8},{10,11... | collective-permute-start | bytes 1179656 | tf_op jit(solution)/shard_map/ppermute | solution.py:13
  77.1 1.3 %copy-start.2 = (f32[2048,256]{0,1:T(8,128)}, f32[2048,256]{0,1:T(8,128)S(1)}, u32[]{:S(2)}) copy-start(f32[2048,256]{0,1:T(8,128)S(1)} %fusion.1) | copy-start | bytes 6291460
where the time goes:
time: 88.4 us; the launch traced here: 87.1 us
  matrix products  28.6 us (32%)
  other arithmetic  18 us (20%)
  waiting for transfers between devices  16.2 us (18%)
  local copies, waits for them, and re-layouts  14.9 us (17%)
  starting transfers between devices  7.5 us (8%)
  between operations  1.8 us (2%)
    dot_general x18, matrix products, dot(): lax.dot_general(a, b, (dims, ((), ())), precision=precision, preferred_el...  28.6 us
    ppermute x5, waiting for transfers between devices, swapped(): return lax.ppermute(value, 'leaf', pairs)  16.2 us
    unnamed x33, local copies, waits for them, and re-layouts  9.1 us
    ppermute x5, starting transfers between devices, swapped(): return lax.ppermute(value, 'leaf', pairs)  7.5 us
    mul x2, other arithmetic, body(): basis = coeff_basis.reshape(levels * rank, row_count) * live[None, :]  4.95 us
    unnamed x4, other arithmetic  4.01 us
    add x3, other arithmetic, tree(): g_own = (g_own + g_sib)[rank:, rank:]  2.11 us
    slice x6, local copies, waits for them, and re-layouts, tree(): response = jnp.concatenate([g_own[rank:, :rank], g_sib[rank:, :rank]], 1)  1.91 us
  transfers between devices with their start and end apart: 5, of which 3 were waited for; matrix products, arithmetic and copies ran while one was open for 9% of the time, Pallas kernels for 0%

commit v1 on v0

v1 whole, which is shorter than its diff:
```python
import functools
import math

import jax
import jax.numpy as jnp
from jax import lax
from jax.experimental import pallas as pl
from jax.experimental.pallas import tpu as pltpu
from jax.sharding import PartitionSpec as P

MESH = pl.DeviceIdType.MESH
HI = lax.Precision.HIGHEST
MID = lax.Precision.HIGH


def swapped(value, bit):
    mask = 2**bit
    pairs = [(source, source ^ mask) for source in range(lax.axis_size("leaf"))]
    return lax.ppermute(value, "leaf", pairs)


def dot(a, b, dims=((1,), (0,)), precision=MID):
    return lax.dot_general(
        a, b, (dims, ((), ())), precision=precision, preferred_element_type=jnp.float32
    )


def tree_kernel(
    levels, rank, base, s_ref, k_ref, g_ref, node_ref, z_out, l_out, k_out, *scratch
):
    inverse = scratch[0]
    own = [None] + [scratch[1 + 3 * n : 4 + 3 * n] for n in range(levels - 1)]
    start = 1 + 3 * (levels - 1)
    got = [scratch[start + 3 * n : start + 3 * n + 3] for n in range(levels)]
    start += 3 * levels
    packed, other, node_sem, send_sem, recv_sem = scratch[start:]
    cols = s_ref.shape[1]
    half = cols // 2
    position = lax.axis_index("leaf")

    def bit_of(height):
        return lax.rem(lax.div(position, 2 ** (base + height)), 2)

    def partner(height):
        return position + (1 - 2 * bit_of(height)) * 2 ** (base + height)

    fetches = []
    for height in range(levels):
        offset = 2**levels - 2 ** (levels - height)
        node = offset + lax.div(position, 2 ** (base + height + 1))
        fetch = pltpu.make_async_copy(node_ref.at[node], inverse.at[height], node_sem.at[height])
        fetch.start()
        fetches.append(fetch)

    barrier = pltpu.get_barrier_semaphore()
    for height in range(levels):
        pl.semaphore_signal(
            barrier, inc=1, device_id={"leaf": partner(height)}, device_id_type=MESH
        )
    pl.semaphore_wait(barrier, levels)

    def send(source, target, height, slot):
        copy = pltpu.make_async_remote_copy(
            src_ref=source,
            dst_ref=target,
            send_sem=send_sem.at[slot],
            recv_sem=recv_sem.at[slot],
            device_id={"leaf": partner(height)},
            device_id_type=MESH,
        )
        copy.start()
        return copy

    mine = bit_of(0)
    keep = pl.ds(pl.multiple_of(mine * half, half), half)
    give = pl.ds(pl.multiple_of((1 - mine) * half, half), half)
    s_now, k_now, g_now = s_ref.at[:, keep], k_ref.at[:, keep], g_ref
    copies = [
        send(s_ref.at[:, give], got[0][0], 0, 0),
        send(g_ref, got[0][1], 0, 1),
        send(k_ref.at[:, give], got[0][2], 0, 2),
    ]
    z_own, z_sib = [], []
    for height in range(levels):
        shift = rank * height - rank * height // 128 * 128
        s_got, g_got, k_got = got[height]
        copies[0].wait_recv()
        lower = bit_of(height) == 0
        here, there = s_now[:rank, :], s_got[:rank, :]
        pair = jnp.concatenate(
            [jnp.where(lower, here, there), jnp.where(lower, there, here)], 0
        )
        fetches[height].wait()
        z = dot(inverse[height], pair, precision=HI)
        z_own.append(jnp.where(lower, z[:rank], z[rank:]))
        z_sib.append(jnp.where(lower, z[rank:], z[:rank]))
        copies[1].wait_recv()
        if height < levels - 1:
            s_next, g_next, k_next = own[height + 1]
            block = slice(shift, shift + rank)
            s_next[...] = (
                s_now[rank:, :]
                + s_got[rank:, :]
                - dot(g_now[rank:, :][:, block], z_own[-1], precision=HI)
                - dot(g_got[rank:, :][:, block], z_sib[-1], precision=HI)
            )
            later = [send(s_next, got[height + 1][0], height + 1, 3 * height + 3)]
            skip = g_now.shape[1] - g_next.shape[1]
            g_next[...] = g_now[rank:, skip:] + g_got[rank:, skip:]
            later.append(send(g_next, got[height + 1][1], height + 1, 3 * height + 4))
        copies[2].wait_recv()
        if height < levels - 1:
            k_next[...] = k_now[rank:, :] + k_got[rank:, :]
            later.append(send(k_next, got[height + 1][2], height + 1, 3 * height + 5))
        for copy in copies:
            copy.wait_send()
        if height < levels - 1:
            copies = later
            s_now, g_now, k_now = own[height + 1]

    rows = levels * rank
    scale = 1.0 / math.sqrt(cols)
    z_all = jnp.concatenate(z_own, 0)
    packed[:rank, :] = z_sib[0]
    packed[rank:rows, :] = z_all[rank:]
    l_list = []
    for height in range(levels):
        shift = rank * height - rank * height // 128 * 128
        chain = jnp.concatenate([z_sib[height]] + z_own[height + 1 :], 0)
        row = got[height][1][:rank, :][:, shift:]
        l_list.append((got[height][0][:rank, :] - dot(row, chain, precision=HI)) * scale)
    l_first = (s_ref[:rank, keep] - dot(g_ref[:rank, :], z_all, precision=HI)) * scale
    packed[rows : rows + rank, :] = l_first
    packed[2 * rows : 2 * rows + rank, :] = k_ref[:rank, keep] * scale
    z_out[:, keep] = z_all
    for height in range(levels):
        part = slice(height * rank, (height + 1) * rank)
        k_part = got[height][2][:rank, :] * scale
        l_out[part, keep] = l_list[height]
        k_out[part, keep] = k_part
        if height > 0:
            packed[rows + height * rank : rows + (height + 1) * rank, :] = l_list[height]
            packed[2 * rows + height * rank : 2 * rows + (height + 1) * rank, :] = k_part
    last = send(packed, other, 0, 3 * levels)
    last.wait_recv()
    z_out[:, give] = other[:rows, :]
    l_out[:, give] = other[rows : 2 * rows, :]
    k_out[:, give] = other[2 * rows :, :]
    last.wait_send()


def tree(sums, weight_sums, gram, node_inverse, levels, rank, base):
    rows, cols = sums.shape
    half = cols // 2
    own, got = [], []
    for height in range(levels):
        left = rows - rank * height
        wide = rows - rank * height // 128 * 128
        group = [
            pltpu.VMEM((left, half), jnp.float32),
            pltpu.VMEM((left, wide), jnp.float32),
            pltpu.VMEM((left, half), jnp.float32),
        ]
        got += group
        if height > 0:
            own += group
    count = 3 * levels + 1
    vmem = pl.BlockSpec(memory_space=pltpu.VMEM)
    return pl.pallas_call(
        functools.partial(tree_kernel, levels, rank, base),
        out_shape=[jax.ShapeDtypeStruct((rows, cols), jnp.float32)] * 3,
        in_specs=[vmem] * 3 + [pl.BlockSpec(memory_space=pl.ANY)],
        out_specs=[vmem] * 3,
        scratch_shapes=[pltpu.VMEM((levels,) + node_inverse.shape[1:], jnp.float32)]
        + own
        + got
        + [
            pltpu.VMEM((3 * rows, half), jnp.float32),
            pltpu.VMEM((3 * rows, half), jnp.float32),
            pltpu.SemaphoreType.DMA((levels,)),
            pltpu.SemaphoreType.DMA((count,)),
            pltpu.SemaphoreType.DMA((count,)),
        ],
        compiler_params=pltpu.CompilerParams(collective_id=0, has_side_effects=True),
    )(sums, weight_sums, gram, node_inverse)


def body(right_side, cotangent, coeff_basis, saved_basis, node_inverse, leaf_rows):
    row_count = right_side.shape[0]
    levels, rank = coeff_basis.shape[0], coeff_basis.shape[1]
    base = lax.axis_size("leaf").bit_length() - 1 - levels
    live = (jnp.arange(row_count, dtype=jnp.int32) < leaf_rows[0]).astype(jnp.float32)
    basis = coeff_basis.reshape(levels * rank, row_count) * live[None, :]
    saved = saved_basis.reshape(levels * rank, row_count)
    sums = dot(basis, right_side)
    weight_sums = dot(basis, cotangent)
    gram = dot(basis, saved, ((1,), (1,)))
    for bit in range(base):
        sums = sums + swapped(sums, bit)
        weight_sums = weight_sums + swapped(weight_sums, bit)
        gram = gram + swapped(gram, bit)
    z_own, l_sib, k_sib = tree(sums, weight_sums, gram, node_inverse, levels, rank, base)
    current = (right_side - dot(saved, z_own, ((0,), (0,)))) * live[:, None]
    left = dot(l_sib, cotangent, ((1,), (1,))) * live[None, :]
    right = dot(k_sib, current, ((1,), (1,)))
    shape = (levels, rank, row_count)
    return (
        current,
        left.astype(jnp.bfloat16).reshape(shape),
        right.astype(jnp.bfloat16).reshape(shape),
    )


def solution(mesh):
    in_specs = (
        P(("groups", "leaf"), None),
        P(("groups", "leaf"), None),
        P(None, None, ("groups", "leaf")),
        P(None, None, ("groups", "leaf")),
        P("groups", None, None),
        P(("groups", "leaf")),
    )
    out_specs = (
        P(("groups", "leaf"), None),
        P(None, None, ("groups", "leaf")),
        P(None, None, ("groups", "leaf")),
    )
    return jax.shard_map(body, mesh=mesh, in_specs=in_specs, out_specs=out_specs, check_vma=False)
```

time: 88.4 us -> 56 us (0.63); the launches traced: 87.1 us -> 55.7 us
  Pallas kernels: 0 us -> 30.3 us
  waiting for transfers between devices: 16.2 us -> 0 us
  other arithmetic: 18 us -> 2.26 us
  matrix products: 28.6 us -> 14.1 us
  starting transfers between devices: 7.5 us -> 0 us
  local copies, waits for them, and re-layouts: 14.9 us -> 7.45 us
    pallas_call x0 -> x1, Pallas kernels: none -> 30.3 us  [tree(): pl.pallas_call(functools.partial(tree_kernel, levels, rank, base), out_sh...]
    ppermute x5 -> x0, waiting for transfers between devices: 16.2 us -> none  [swapped(): return lax.ppermute(value, 'leaf', pairs)]
    dot_general x18 -> x6, matrix products: 28.6 us -> 14.1 us  [dot(): lax.dot_general(a, b, (dims, ((), ())), precision=precision, preferred_el...]
    ppermute x5 -> x0, starting transfers between devices: 7.5 us -> none  [swapped(): return lax.ppermute(value, 'leaf', pairs)]
    slice x17 -> x0, local copies, waits for them, and re-layouts: 5.8 us -> none  [the longest x6 1.91 us: tree(): response = jnp.concatenate([g_own[rank:, :rank], g_sib[rank:, :rank]], 1)]
    unnamed x4 -> x0, other arithmetic: 4.01 us -> none
    concatenate x9 -> x0, other arithmetic: 4 us -> none  [the longest x4 1.7 us: tree(): jnp.roll(inverse, (rank, rank), (0, 1))]
    add x6 -> x0, other arithmetic: 3.87 us -> none  [the longest x3 2.11 us: tree(): g_own = (g_own + g_sib)[rank:, rank:]]
  transfers between devices with their start and end apart: 5 -> 0, of which waited for: 3 -> 0; matrix products, arithmetic and copies ran while one was open for 9% -> 0% of each run, Pallas kernels for 0% -> 0%
where the time goes in v1:
time: 56 us; the launch traced here: 55.7 us
  Pallas kernels  30.3 us (54%)
  matrix products  14.1 us (25%)
  local copies, waits for them, and re-layouts  7.45 us (13%)
  other arithmetic  2.26 us (4%)
  between operations  1.51 us (3%)
    pallas_call x1, Pallas kernels, tree(): pl.pallas_call(functools.partial(tree_kernel, levels, rank, base), out_sh...  30.3 us
    dot_general x6, matrix products, dot(): lax.dot_general(a, b, (dims, ((), ())), precision=precision, preferred_el...  14.1 us
    unnamed x18, local copies, waits for them, and re-layouts  7.45 us
    mul x2, other arithmetic, body(): basis = coeff_basis.reshape(levels * rank, row_count) * live[None, :]  2.26 us

profile of v1, /device:TPU:0, one launch (start us, length us, event | category | flops | bytes accessed | tf_op | source)
XLA Modules:
  0.0 55.7 jit_solution(17319484784851578936)
XLA Ops:
  0.6 0.0 copy-start
  1.5 0.0 copy-start.3
  1.5 2.0 %bitcast_multiply_fusion = f32[256,2048]{1,0:T(8,128)S(1)} fusion(f32[4,64,2048]{2,1,0:T(8,128)} %param.8, f32[2048]{0:T(1024)S(1)} %fusion.3), kind=kLoop, calls=%fused_computation.6 | loop fusion | flops 524288 | bytes 4202496 | tf_op jit(solution)/shard_map/mul | solution.py:193
  3.4 0.2 copy-done.3
  3.7 0.0 copy-start.4
  3.7 1.9 %fusion.4.s_ref = f32[256,256]{1,0:T(8,128)} fusion(f32[256,2048]{1,0:T(8,128)S(1)} %bitcast_multiply_fusion, f32[2048,256]{1,0:T(8,128)S(1)} %copy-done.3), kind=kOutput, calls=%fused_computation.10 | convolution fusion | flops 805306368 | bytes 4456448 | tf_op jit(solution)/shard_map/dot_general | solution.py:23
  5.5 0.0 copy-done.4
  5.5 0.0 copy-start.2
  5.5 1.9 %fusion.5.k_ref = f32[256,256]{1,0:T(8,128)} fusion(f32[256,2048]{1,0:T(8,128)S(1)} %bitcast_multiply_fusion, f32[2048,256]{1,0:T(8,128)S(1)} %copy-done.4), kind=kOutput, calls=%fused_computation.11 | convolution fusion | flops 805306368 | bytes 4456448 | tf_op jit(solution)/shard_map/dot_general | solution.py:23
  7.4 0.0 copy-done.2
  7.4 0.3 broadcast_multiply_fusion
  7.7 0.0 copy-done
  7.7 1.8 %fusion.6.g_ref = f32[256,256]{1,0:T(8,128)} fusion(f32[256,2048]{1,0:T(8,128)S(1)} %bitcast.28, f32[256,2048]{1,0:T(8,128)S(1)} %bitcast.26), kind=kOutput, calls=%fused_computation.12 | convolution fusion | flops 805306368 | bytes 4456448 | tf_op jit(solution)/shard_map/dot_general | solution.py:23
  9.5 30.3 %shard_map.85 = (f32[256,256]{1,0:T(8,128)}, f32[256,256]{1,0:T(8,128)}, f32[256,256]{1,0:T(8,128)}) custom-call(f32[256,256]{1,0:T(8,128)} %fusion.4.s_ref, f32[256,256]{1,0:T(8,128)} %fusion.5.k_ref, f32[256,256]{1,0:T(8,128)} %fusion.6.g_ref, f32[15,128,128]{2,1,0:T(8,128)} %node_ref.1), custom_call_target="tpu_custom_call" | custom-call | tf_op jit(solution)/shard_map/pallas_call | solution.py:169
  39.8 0.0 copy-start.5
  39.9 2.9 %copy.9 = f32[2048,256]{0,1:T(8,128)} copy(f32[2048,256]{1,0:T(8,128)} %param.6) | data formatting | bytes 4194304 | tf_op args[0]
  42.8 0.0 copy-done.5
  42.8 0.0 copy-start.7
  42.8 2.9 %fusion.1 = f32[2048,256]{0,1:T(8,128)S(1)} fusion(f32[2048,256]{0,1:T(8,128)} %copy.9, f32[256,256]{1,0:T(8,128)S(1)} %copy-done.5, f32[256,2048]{1,0:T(8,128)S(1)} %bitcast.27, f32[2048]{0:T(1024)S(1)} %fusion.3), kind=kOutput, calls=%fused_computation.3 | convolution fusion | flops 806354944 | bytes 6561792 | tf_op jit(solution)/shard_map/dot_general | solution.py:23
  45.6 0.0 copy-start.1
  45.7 1.3 %copy-done.1 = f32[2048,256]{0,1:T(8,128)} copy-done((f32[2048,256]{0,1:T(8,128)}, f32[2048,256]{0,1:T(8,128)S(1)}, u32[]{:S(2)}) %copy-start.1) | copy-done | bytes 2097176
  47.0 0.0 copy-done.7
  47.0 2.2 %convolution_convert_fusion = bf16[256,2048]{1,0:T(8,128)(2,1)} fusion(f32[256,256]{1,0:T(8,128)S(1)} %copy-done.7, f32[2048,256]{0,1:T(8,128)S(1)} %fusion.1), kind=kOutput, calls=%fused_computation.5 | convolution fusion | flops 805830656 | bytes 3407872 | tf_op jit(solution)/shard_map/dot_general | solution.py:23
  49.1 0.0 copy-start.6
  49.2 2.9 %copy.10 = f32[2048,256]{1,0:T(8,128)} copy(f32[2048,256]{0,1:T(8,128)} %copy-done.1) | data formatting | bytes 4194304
  52.1 0.0 copy-done.6
  52.1 3.6 %fusion.2 = bf16[256,2048]{1,0:T(8,128)(2,1)} fusion(f32[256,256]{1,0:T(8,128)S(1)} %copy-done.6, f32[2048,256]{1,0:T(8,128)} %param.7, f32[2048]{0:T(1024)S(1)} %fusion.3), kind=kOutput, calls=%fused_computation.4 | convolution fusion | flops 806354944 | bytes 3416064 | tf_op jit(solution)/shard_map/dot_general | solution.py:23
  (1 shorter events, 0.0 us)
Async XLA Ops:
  0.6 7.1 %copy-start = (f32[4,64,2048]{2,1,0:T(8,128)S(1)}, f32[4,64,2048]{2,1,0:T(8,128)}, u32[]{:S(2)}) copy-start(f32[4,64,2048]{2,1,0:T(8,128)} %param.9) | copy-start | bytes 6291460
  1.5 2.2 %copy-start.3 = (f32[2048,256]{1,0:T(8,128)S(1)}, f32[2048,256]{1,0:T(8,128)}, u32[]{:S(2)}) copy-start(f32[2048,256]{1,0:T(8,128)} %param.6) | copy-start | bytes 6291460
  3.7 1.9 %copy-start.4 = (f32[2048,256]{1,0:T(8,128)S(1)}, f32[2048,256]{1,0:T(8,128)}, u32[]{:S(2)}) copy-start(f32[2048,256]{1,0:T(8,128)} %param.7) | copy-start | bytes 6291460
  5.5 1.9 %copy-start.2 = (f32[4,64,2048]{2,1,0:T(8,128)S(1)}, f32[4,64,2048]{2,1,0:T(8,128)}, u32[]{:S(2)}) copy-start(f32[4,64,2048]{2,1,0:T(8,128)} %param.8) | copy-start | bytes 6291460
  39.8 2.9 %copy-start.5 = (f32[256,256]{1,0:T(8,128)S(1)}, f32[256,256]{1,0:T(8,128)}, u32[]{:S(2)}) copy-start(f32[256,256]{1,0:T(8,128)} %get-tuple-element.6) | copy-start | bytes 786436
  42.8 4.2 %copy-start.7 = (f32[256,256]{1,0:T(8,128)S(1)}, f32[256,256]{1,0:T(8,128)}, u32[]{:S(2)}) copy-start(f32[256,256]{1,0:T(8,128)} %get-tuple-element.8) | copy-start | bytes 786436
  45.6 1.3 %copy-start.1 = (f32[2048,256]{0,1:T(8,128)}, f32[2048,256]{0,1:T(8,128)S(1)}, u32[]{:S(2)}) copy-start(f32[2048,256]{0,1:T(8,128)S(1)} %fusion.1) | copy-start | bytes 6291460
  49.1 2.9 %copy-start.6 = (f32[256,256]{1,0:T(8,128)S(1)}, f32[256,256]{1,0:T(8,128)}, u32[]{:S(2)}) copy-start(f32[256,256]{1,0:T(8,128)} %get-tuple-element.7) | copy-start | bytes 786436

commit v2 on v1

--- a/solution.py
+++ b/solution.py
@@ -10,7 +10,7 @@
 
 MESH = pl.DeviceIdType.MESH
 HI = lax.Precision.HIGHEST
-MID = lax.Precision.HIGH
+TILE = 512
 
 
 def swapped(value, bit):
@@ -19,7 +19,7 @@
     return lax.ppermute(value, "leaf", pairs)
 
 
-def dot(a, b, dims=((1,), (0,)), precision=MID):
+def dot(a, b, dims=((1,), (0,)), precision=HI):
     return lax.dot_general(
         a, b, (dims, ((), ())), precision=precision, preferred_element_type=jnp.float32
     )
@@ -185,30 +185,99 @@
     )(sums, weight_sums, gram, node_inverse)
 
 
+def split(value):
+    high = value.astype(jnp.bfloat16)
+    return high, (value - high.astype(jnp.float32)).astype(jnp.bfloat16)
+
+
+def triple(left, right, dims):
+    def one(a, b):
+        return lax.dot_general(a, b, (dims, ((), ())), preferred_element_type=jnp.float32)
+
+    return one(left[0], right[1]) + one(left[1], right[0]) + one(left[0], right[0])
+
+
+def lead_kernel(rows_ref, right_ref, cot_ref, basis_ref, saved_ref, s_ref, k_ref, g_ref):
+    step = pl.program_id(0)
+    tile = basis_ref.shape[1]
+    place = step * tile + lax.broadcasted_iota(jnp.int32, (1, tile), 1)
+    basis = split(jnp.where(place < rows_ref[0], basis_ref[...], 0.0))
+    s_now = triple(basis, split(right_ref[...]), ((1,), (0,)))
+    k_now = triple(basis, split(cot_ref[...]), ((1,), (0,)))
+    g_now = triple(basis, split(saved_ref[...]), ((1,), (1,)))
+
+    @pl.when(step == 0)
+    def _():
+        s_ref[...] = s_now
+        k_ref[...] = k_now
+        g_ref[...] = g_now
+
+    @pl.when(step > 0)
+    def _():
+        s_ref[...] += s_now
+        k_ref[...] += k_now
+        g_ref[...] += g_now
+
+
+def close_kernel(
+    rows_ref, right_ref, cot_ref, saved_ref, z_ref, l_ref, k_ref, x_ref, left_ref, grad_ref
+):
+    tile = saved_ref.shape[1]
+    first = pl.program_id(0) * tile
+    down = first + lax.broadcasted_iota(jnp.int32, (tile, 1), 0)
+    across = first + lax.broadcasted_iota(jnp.int32, (1, tile), 1)
+    moved = triple(split(saved_ref[...]), split(z_ref[...]), ((0,), (0,)))
+    solved = jnp.where(down < rows_ref[0], right_ref[...] - moved, 0.0)
+    x_ref[...] = solved
+    left = triple(split(l_ref[...]), split(cot_ref[...]), ((1,), (1,)))
+    left_ref[...] = jnp.where(across < rows_ref[0], left, 0.0).astype(jnp.bfloat16)
+    grad = triple(split(k_ref[...]), split(solved), ((1,), (1,)))
+    grad_ref[...] = grad.astype(jnp.bfloat16)
+
+
 def body(right_side, cotangent, coeff_basis, saved_basis, node_inverse, leaf_rows):
-    row_count = right_side.shape[0]
+    row_count, cols = right_side.shape
     levels, rank = coeff_basis.shape[0], coeff_basis.shape[1]
+    height = levels * rank
     base = lax.axis_size("leaf").bit_length() - 1 - levels
-    live = (jnp.arange(row_count, dtype=jnp.int32) < leaf_rows[0]).astype(jnp.float32)
-    basis = coeff_basis.reshape(levels * rank, row_count) * live[None, :]
-    saved = saved_basis.reshape(levels * rank, row_count)
-    sums = dot(basis, right_side)
-    weight_sums = dot(basis, cotangent)
-    gram = dot(basis, saved, ((1,), (1,)))
+    basis = coeff_basis.reshape(height, row_count)
+    saved = saved_basis.reshape(height, row_count)
+    tile = math.gcd(row_count, TILE)
+    grid = (row_count // tile,)
+    count = pl.BlockSpec(memory_space=pltpu.SMEM)
+    tall = pl.BlockSpec((tile, cols), lambda i: (i, 0))
+    wide = pl.BlockSpec((height, tile), lambda i: (0, i))
+    small = pl.BlockSpec((height, cols), lambda i: (0, 0))
+    square = pl.BlockSpec((height, height), lambda i: (0, 0))
+    sums, weight_sums, gram = pl.pallas_call(
+        lead_kernel,
+        grid=grid,
+        out_shape=[
+            jax.ShapeDtypeStruct((height, cols), jnp.float32),
+            jax.ShapeDtypeStruct((height, cols), jnp.float32),
+            jax.ShapeDtypeStruct((height, height), jnp.float32),
+        ],
+        in_specs=[count, tall, tall, wide, wide],
+        out_specs=[small, small, square],
+    )(leaf_rows, right_side, cotangent, basis, saved)
     for bit in range(base):
         sums = sums + swapped(sums, bit)
         weight_sums = weight_sums + swapped(weight_sums, bit)
         gram = gram + swapped(gram, bit)
     z_own, l_sib, k_sib = tree(sums, weight_sums, gram, node_inverse, levels, rank, base)
-    current = (right_side - dot(saved, z_own, ((0,), (0,)))) * live[:, None]
-    left = dot(l_sib, cotangent, ((1,), (1,))) * live[None, :]
-    right = dot(k_sib, current, ((1,), (1,)))
+    current, left, right = pl.pallas_call(
+        close_kernel,
+        grid=grid,
+        out_shape=[
+            jax.ShapeDtypeStruct((row_count, cols), jnp.float32),
+            jax.ShapeDtypeStruct((height, row_count), jnp.bfloat16),
+            jax.ShapeDtypeStruct((height, row_count), jnp.bfloat16),
+        ],
+        in_specs=[count, tall, tall, wide, small, small, small],
+        out_specs=[tall, wide, wide],
+    )(leaf_rows, right_side, cotangent, saved, z_own, l_sib, k_sib)
     shape = (levels, rank, row_count)
-    return (
-        current,
-        left.astype(jnp.bfloat16).reshape(shape),
-        right.astype(jnp.bfloat16).reshape(shape),
-    )
+    return current, left.reshape(shape), right.reshape(shape)
 
 
 def solution(mesh):

time: 56 us -> 45.5 us (0.81)
  matrix products: 14.1 us -> 0 us
  Pallas kernels: 30.3 us -> 43.9 us
  local copies, waits for them, and re-layouts: 7.45 us -> 0 us
  other arithmetic: 2.26 us -> 0 us
    dot_general x6 -> x0, matrix products: 14.1 us -> none  [dot(): lax.dot_general(a, b, (dims, ((), ())), precision=precision, preferred_el...]
    pallas_call x0 -> x2, Pallas kernels: none -> 13.6 us  [the longest x1 6.95 us: body(): pl.pallas_call(close_kernel, grid=grid, out_shape=[jax.ShapeDtypeStruct((...]
    unnamed x18 -> x0, local copies, waits for them, and re-layouts: 7.45 us -> none
    mul x2 -> x0, other arithmetic: 2.26 us -> none  [body(): basis = coeff_basis.reshape(levels * rank, row_count) * live[None, :]]
where the time goes in v2:
time: 45.5 us; the launch traced here: 45.2 us
  Pallas kernels  43.9 us (96%)
  between operations  1.29 us (3%)
    pallas_call x1, Pallas kernels, tree(): pl.pallas_call(functools.partial(tree_kernel, levels, rank, base), out_sh...  30.3 us
    pallas_call x1, Pallas kernels, body(): pl.pallas_call(close_kernel, grid=grid, out_shape=[jax.ShapeDtypeStruct((...  6.95 us
    pallas_call x1, Pallas kernels, body(): pl.pallas_call(lead_kernel, grid=grid, out_shape=[jax.ShapeDtypeStruct((h...  6.69 us

profile of v2, /device:TPU:0, one launch (start us, length us, event | category | flops | bytes accessed | tf_op | source)
XLA Modules:
  0.0 45.2 jit_solution(3527966794146946292)
XLA Ops:
  1.3 6.7 %shard_map.85 = (f32[256,256]{1,0:T(8,128)}, f32[256,256]{1,0:T(8,128)}, f32[256,256]{1,0:T(8,128)}) custom-call(s32[1]{0:T(128)S(6)} %copy.9.rows_ref, f32[2048,256]{1,0:T(8,128)} %right_ref.3, f32[2048,256]{1,0:T(8,128)} %cot_ref.3, f32[256,2048]{1,0:T(8,128)} %bitcast.6, f32[256,2048]{1,0:T(8,128)} %bitcast.4), custom_call_target="tpu_custom_call" | custom-call | tf_op jit(solution)/shard_map/pallas_call | solution.py:252
  8.0 30.3 %shard_map.86 = (f32[256,256]{1,0:T(8,128)}, f32[256,256]{1,0:T(8,128)}, f32[256,256]{1,0:T(8,128)}) custom-call(f32[256,256]{1,0:T(8,128)} %get-tuple-element.12.s_ref, f32[256,256]{1,0:T(8,128)} %get-tuple-element.13.k_ref, f32[256,256]{1,0:T(8,128)} %get-tuple-element.14.g_ref, f32[15,128,128]{2,1,0:T(8,128)} %node_ref.1), custom_call_target="tpu_custom_call" | custom-call | tf_op jit(solution)/shard_map/pallas_call | solution.py:169
  38.3 7.0 %shard_map.87 = (f32[2048,256]{1,0:T(8,128)}, bf16[256,2048]{1,0:T(8,128)(2,1)}, bf16[256,2048]{1,0:T(8,128)(2,1)}) custom-call(s32[1]{0:T(128)S(6)} %copy.9.rows_ref, f32[2048,256]{1,0:T(8,128)} %right_ref.3, f32[2048,256]{1,0:T(8,128)} %cot_ref.3, f32[256,2048]{1,0:T(8,128)} %bitcast.5, f32[256,256]{1,0:T(8,128)} %get-tuple-element.15.z_ref, ...), custom_call_target="tpu_custom_call" | custom-call | tf_op jit(solution)/shard_map/pallas_call | solution.py:268

commit v3 on v2

--- a/solution.py
+++ b/solution.py
@@ -27,6 +27,96 @@
 
 def tree_kernel(
     levels, rank, base, s_ref, k_ref, g_ref, node_ref, z_out, l_out, k_out, *scratch
+):
+    steps = [lambda: None] * 3
+    tree_steps(
+        levels, rank, base, steps, s_ref, k_ref, g_ref, node_ref, z_out, l_out, k_out, scratch
+    )
+
+
+def whole_kernel(
+    levels,
+    rank,
+    tile,
+    rows_ref,
+    right_ref,
+    cot_ref,
+    basis_ref,
+    saved_ref,
+    node_ref,
+    z_out,
+    l_out,
+    k_out,
+    s_ref,
+    k_ref,
+    g_ref,
+    right_in,
+    cot_in,
+    basis_in,
+    saved_in,
+    high_ref,
+    low_ref,
+    load_sem,
+    *scratch,
+):
+    tiles = basis_ref.shape[1] // tile
+
+    def load(source, target, kind, axis):
+        copies = []
+        for n in range(tiles):
+            part = pl.ds(n * tile, tile)
+            index = (part, slice(None)) if axis == 0 else (slice(None), part)
+            copies.append(
+                pltpu.make_async_copy(source.at[index], target.at[index], load_sem.at[kind, n])
+            )
+        return copies
+
+    basis_loads = load(basis_ref, basis_in, 0, 1)
+    saved_loads = load(saved_ref, saved_in, 1, 1)
+    right_loads = load(right_ref, right_in, 2, 0)
+    cot_loads = load(cot_ref, cot_in, 3, 0)
+    for one, two in zip(basis_loads, saved_loads):
+        one.start()
+        two.start()
+    for one in right_loads + cot_loads:
+        one.start()
+
+    def gram_step():
+        total = None
+        for n in range(tiles):
+            part = slice(n * tile, (n + 1) * tile)
+            place = n * tile + lax.broadcasted_iota(jnp.int32, (1, tile), 1)
+            basis_loads[n].wait()
+            high, low = split(jnp.where(place < rows_ref[0], basis_in[:, part], 0.0))
+            high_ref[:, part] = high
+            low_ref[:, part] = low
+            saved_loads[n].wait()
+            term = triple((high, low), split(saved_in[:, part]), ((1,), (1,)))
+            total = term if total is None else total + term
+        g_ref[...] = total
+
+    def column_step(loads, source, target):
+        total = None
+        for n in range(tiles):
+            part = slice(n * tile, (n + 1) * tile)
+            loads[n].wait()
+            basis = (high_ref[:, part], low_ref[:, part])
+            term = triple(basis, split(source[part, :]), ((1,), (0,)))
+            total = term if total is None else total + term
+        target[...] = total
+
+    steps = [
+        gram_step,
+        lambda: column_step(right_loads, right_in, s_ref),
+        lambda: column_step(cot_loads, cot_in, k_ref),
+    ]
+    tree_steps(
+        levels, rank, 0, steps, s_ref, k_ref, g_ref, node_ref, z_out, l_out, k_out, scratch
+    )
+
+
+def tree_steps(
+    levels, rank, base, steps, s_ref, k_ref, g_ref, node_ref, z_out, l_out, k_out, scratch
 ):
     inverse = scratch[0]
     own = [None] + [scratch[1 + 3 * n : 4 + 3 * n] for n in range(levels - 1)]
@@ -57,6 +147,7 @@
         pl.semaphore_signal(
             barrier, inc=1, device_id={"leaf": partner(height)}, device_id_type=MESH
         )
+    steps[0]()
     pl.semaphore_wait(barrier, levels)
 
     def send(source, target, height, slot):
@@ -74,17 +165,36 @@
     mine = bit_of(0)
     keep = pl.ds(pl.multiple_of(mine * half, half), half)
     give = pl.ds(pl.multiple_of((1 - mine) * half, half), half)
-    s_now, k_now, g_now = s_ref.at[:, keep], k_ref.at[:, keep], g_ref
-    copies = [
-        send(s_ref.at[:, give], got[0][0], 0, 0),
-        send(g_ref, got[0][1], 0, 1),
-        send(k_ref.at[:, give], got[0][2], 0, 2),
-    ]
+    s_all = [s_ref.at[:, keep]] + [own[n][0] for n in range(1, levels)]
+    g_all = [g_ref] + [own[n][1] for n in range(1, levels)]
+    k_all = [k_ref.at[:, keep]] + [own[n][2] for n in range(1, levels)]
+    sends = []
+
+    def advance_gram(height, copy):
+        copy.wait_recv()
+        if height == levels - 1:
+            return None
+        g_now, g_got, g_next = g_all[height], got[height][1], g_all[height + 1]
+        skip = g_now.shape[1] - g_next.shape[1]
+        g_next[...] = g_now[rank:, skip:] + g_got[rank:, skip:]
+        sends.append(send(g_next, got[height + 1][1], height + 1, 3 * height + 4))
+        return sends[-1]
+
+    g_copy = send(g_ref, got[0][1], 0, 1)
+    sends.append(g_copy)
+    steps[1]()
+    s_copy = send(s_ref.at[:, give], got[0][0], 0, 0)
+    sends.append(s_copy)
+    g_copy = advance_gram(0, g_copy)
+    steps[2]()
+    k_copy = send(k_ref.at[:, give], got[0][2], 0, 2)
+    sends.append(k_copy)
     z_own, z_sib = [], []
     for height in range(levels):
         shift = rank * height - rank * height // 128 * 128
+        s_now, g_now, k_now = s_all[height], g_all[height], k_all[height]
         s_got, g_got, k_got = got[height]
-        copies[0].wait_recv()
+        s_copy.wait_recv()
         lower = bit_of(height) == 0
         here, there = s_now[:rank, :], s_got[:rank, :]
         pair = jnp.concatenate(
@@ -94,9 +204,8 @@
         z = dot(inverse[height], pair, precision=HI)
         z_own.append(jnp.where(lower, z[:rank], z[rank:]))
         z_sib.append(jnp.where(lower, z[rank:], z[:rank]))
-        copies[1].wait_recv()
         if height < levels - 1:
-            s_next, g_next, k_next = own[height + 1]
+            s_next, _, k_next = own[height + 1]
             block = slice(shift, shift + rank)
             s_next[...] = (
                 s_now[rank:, :]
@@ -104,19 +213,16 @@
                 - dot(g_now[rank:, :][:, block], z_own[-1], precision=HI)
                 - dot(g_got[rank:, :][:, block], z_sib[-1], precision=HI)
             )
-            later = [send(s_next, got[height + 1][0], height + 1, 3 * height + 3)]
-            skip = g_now.shape[1] - g_next.shape[1]
-            g_next[...] = g_now[rank:, skip:] + g_got[rank:, skip:]
-            later.append(send(g_next, got[height + 1][1], height + 1, 3 * height + 4))
-        copies[2].wait_recv()
-        if height < levels - 1:
+            s_copy = send(s_next, got[height + 1][0], height + 1, 3 * height + 3)
+            sends.append(s_copy)
+            k_copy.wait_recv()
             k_next[...] = k_now[rank:, :] + k_got[rank:, :]
-            later.append(send(k_next, got[height + 1][2], height + 1, 3 * height + 5))
-        for copy in copies:
-            copy.wait_send()
-        if height < levels - 1:
-            copies = later
-            s_now, g_now, k_now = own[height + 1]
+            k_copy = send(k_next, got[height + 1][2], height + 1, 3 * height + 5)
+            sends.append(k_copy)
+            g_copy = advance_gram(height + 1, g_copy)
+    k_copy.wait_recv()
+    for copy in sends:
+        copy.wait_send()
 
     rows = levels * rank
     scale = 1.0 / math.sqrt(cols)
@@ -149,8 +255,7 @@
     last.wait_send()
 
 
-def tree(sums, weight_sums, gram, node_inverse, levels, rank, base):
-    rows, cols = sums.shape
+def tree_scratch(levels, rank, rows, cols, node_shape):
     half = cols // 2
     own, got = [], []
     for height in range(levels):
@@ -165,13 +270,8 @@
         if height > 0:
             own += group
     count = 3 * levels + 1
-    vmem = pl.BlockSpec(memory_space=pltpu.VMEM)
-    return pl.pallas_call(
-        functools.partial(tree_kernel, levels, rank, base),
-        out_shape=[jax.ShapeDtypeStruct((rows, cols), jnp.float32)] * 3,
-        in_specs=[vmem] * 3 + [pl.BlockSpec(memory_space=pl.ANY)],
-        out_specs=[vmem] * 3,
-        scratch_shapes=[pltpu.VMEM((levels,) + node_inverse.shape[1:], jnp.float32)]
+    return (
+        [pltpu.VMEM((levels,) + node_shape, jnp.float32)]
         + own
         + got
         + [
@@ -180,9 +280,48 @@
             pltpu.SemaphoreType.DMA((levels,)),
             pltpu.SemaphoreType.DMA((count,)),
             pltpu.SemaphoreType.DMA((count,)),
-        ],
+        ]
+    )
+
+
+def tree(sums, weight_sums, gram, node_inverse, levels, rank, base):
+    rows, cols = sums.shape
+    vmem = pl.BlockSpec(memory_space=pltpu.VMEM)
+    return pl.pallas_call(
+        functools.partial(tree_kernel, levels, rank, base),
+        out_shape=[jax.ShapeDtypeStruct((rows, cols), jnp.float32)] * 3,
+        in_specs=[vmem] * 3 + [pl.BlockSpec(memory_space=pl.ANY)],
+        out_specs=[vmem] * 3,
+        scratch_shapes=tree_scratch(levels, rank, rows, cols, node_inverse.shape[1:]),
         compiler_params=pltpu.CompilerParams(collective_id=0, has_side_effects=True),
     )(sums, weight_sums, gram, node_inverse)
+
+
+def whole_tree(leaf_rows, right_side, cotangent, basis, saved, node_inverse, levels, rank, tile):
+    rows, depth = basis.shape
+    cols = right_side.shape[1]
+    vmem = pl.BlockSpec(memory_space=pltpu.VMEM)
+    remote = pl.BlockSpec(memory_space=pl.ANY)
+    return pl.pallas_call(
+        functools.partial(whole_kernel, levels, rank, tile),
+        out_shape=[jax.ShapeDtypeStruct((rows, cols), jnp.float32)] * 3,
+        in_specs=[pl.BlockSpec(memory_space=pltpu.SMEM)] + [remote] * 5,
+        out_specs=[vmem] * 3,
+        scratch_shapes=[
+            pltpu.VMEM((rows, cols), jnp.float32),
+            pltpu.VMEM((rows, cols), jnp.float32),
+            pltpu.VMEM((rows, rows), jnp.float32),
+            pltpu.VMEM((depth, cols), jnp.float32),
+            pltpu.VMEM((depth, cols), jnp.float32),
+            pltpu.VMEM((rows, depth), jnp.float32),
+            pltpu.VMEM((rows, depth), jnp.float32),
+            pltpu.VMEM((rows, depth), jnp.bfloat16),
+            pltpu.VMEM((rows, depth), jnp.bfloat16),
+            pltpu.SemaphoreType.DMA((4, depth // tile)),
+        ]
+        + tree_scratch(levels, rank, rows, cols, node_inverse.shape[1:]),
+        compiler_params=pltpu.CompilerParams(collective_id=0, has_side_effects=True),
+    )(leaf_rows, right_side, cotangent, basis, saved, node_inverse)
 
 
 def split(value):
@@ -249,22 +388,27 @@
     wide = pl.BlockSpec((height, tile), lambda i: (0, i))
     small = pl.BlockSpec((height, cols), lambda i: (0, 0))
     square = pl.BlockSpec((height, height), lambda i: (0, 0))
-    sums, weight_sums, gram = pl.pallas_call(
-        lead_kernel,
-        grid=grid,
-        out_shape=[
-            jax.ShapeDtypeStruct((height, cols), jnp.float32),
-            jax.ShapeDtypeStruct((height, cols), jnp.float32),
-            jax.ShapeDtypeStruct((height, height), jnp.float32),
-        ],
-        in_specs=[count, tall, tall, wide, wide],
-        out_specs=[small, small, square],
-    )(leaf_rows, right_side, cotangent, basis, saved)
-    for bit in range(base):
-        sums = sums + swapped(sums, bit)
-        weight_sums = weight_sums + swapped(weight_sums, bit)
-        gram = gram + swapped(gram, bit)
-    z_own, l_sib, k_sib = tree(sums, weight_sums, gram, node_inverse, levels, rank, base)
+    if base == 0:
+        z_own, l_sib, k_sib = whole_tree(
+            leaf_rows, right_side, cotangent, basis, saved, node_inverse, levels, rank, tile
+        )
+    else:
+        sums, weight_sums, gram = pl.pallas_call(
+            lead_kernel,
+            grid=grid,
+            out_shape=[
+                jax.ShapeDtypeStruct((height, cols), jnp.float32),
+                jax.ShapeDtypeStruct((height, cols), jnp.float32),
+                jax.ShapeDtypeStruct((height, height), jnp.float32),
+            ],
+            in_specs=[count, tall, tall, wide, wide],
+            out_specs=[small, small, square],
+        )(leaf_rows, right_side, cotangent, basis, saved)
+        for bit in range(base):
+            sums = sums + swapped(sums, bit)
+            weight_sums = weight_sums + swapped(weight_sums, bit)
+            gram = gram + swapped(gram, bit)
+        z_own, l_sib, k_sib = tree(sums, weight_sums, gram, node_inverse, levels, rank, base)
     current, left, right = pl.pallas_call(
         close_kernel,
         grid=grid,

time: 45.5 us -> 39.3 us (0.86)
  Pallas kernels: 43.9 us -> 37.8 us
    pallas_call x2 -> x1, Pallas kernels: 37 us -> 30.9 us  [whole_tree(): pl.pallas_call(functools.partial(whole_kernel, levels, rank, tile), out_s...]
where the time goes in v3:
time: 39.3 us; the launch traced here: 39.1 us
  Pallas kernels  37.8 us (96%)
  between operations  1.29 us (3%)
    pallas_call x1, Pallas kernels, whole_tree(): pl.pallas_call(functools.partial(whole_kernel, levels, rank, tile), out_s...  30.9 us
    pallas_call x1, Pallas kernels, body(): pl.pallas_call(close_kernel, grid=grid, out_shape=[jax.ShapeDtypeStruct((...  6.95 us

profile of v3, /device:TPU:0, one launch (start us, length us, event | category | flops | bytes accessed | tf_op | source)
XLA Modules:
  0.0 39.1 jit_solution(14068859252397507113)
XLA Ops:
  1.3 30.9 %shard_map.85 = (f32[256,256]{1,0:T(8,128)}, f32[256,256]{1,0:T(8,128)}, f32[256,256]{1,0:T(8,128)}) custom-call(s32[1]{0:T(128)S(6)} %copy.9.rows_ref, f32[2048,256]{1,0:T(8,128)} %right_ref.3, f32[2048,256]{1,0:T(8,128)} %cot_ref.3, f32[256,2048]{1,0:T(8,128)} %bitcast.6, f32[256,2048]{1,0:T(8,128)} %bitcast.4, f32[15,128,128]{2,1,0:T(8,128)} %node_ref.1), custom_call_target="tpu_custom_call" | custom-call | tf_op jit(solution)/shard_map/pallas_call | solution.py:305
  32.2 7.0 %shard_map.86 = (f32[2048,256]{1,0:T(8,128)}, bf16[256,2048]{1,0:T(8,128)(2,1)}, bf16[256,2048]{1,0:T(8,128)(2,1)}) custom-call(s32[1]{0:T(128)S(6)} %copy.9.rows_ref, f32[2048,256]{1,0:T(8,128)} %right_ref.3, f32[2048,256]{1,0:T(8,128)} %cot_ref.3, f32[256,2048]{1,0:T(8,128)} %bitcast.5, f32[256,256]{1,0:T(8,128)} %get-tuple-element.9.z_ref, ...), custom_call_target="tpu_custom_call" | custom-call | tf_op jit(solution)/shard_map/pallas_call | solution.py:412

commit v4 on v3

--- a/solution.py
+++ b/solution.py
@@ -9,7 +9,6 @@
 from jax.sharding import PartitionSpec as P
 
 MESH = pl.DeviceIdType.MESH
-HI = lax.Precision.HIGHEST
 TILE = 512
 
 
@@ -19,10 +18,8 @@
     return lax.ppermute(value, "leaf", pairs)
 
 
-def dot(a, b, dims=((1,), (0,)), precision=HI):
-    return lax.dot_general(
-        a, b, (dims, ((), ())), precision=precision, preferred_element_type=jnp.float32
-    )
+def dot(a, b, dims=((1,), (0,))):
+    return triple(split(a), split(b), dims)
 
 
 def tree_kernel(
@@ -201,7 +198,7 @@
             [jnp.where(lower, here, there), jnp.where(lower, there, here)], 0
         )
         fetches[height].wait()
-        z = dot(inverse[height], pair, precision=HI)
+        z = dot(inverse[height], pair)
         z_own.append(jnp.where(lower, z[:rank], z[rank:]))
         z_sib.append(jnp.where(lower, z[rank:], z[:rank]))
         if height < levels - 1:
@@ -210,8 +207,8 @@
             s_next[...] = (
                 s_now[rank:, :]
                 + s_got[rank:, :]
-                - dot(g_now[rank:, :][:, block], z_own[-1], precision=HI)
-                - dot(g_got[rank:, :][:, block], z_sib[-1], precision=HI)
+                - dot(g_now[rank:, :][:, block], z_own[-1])
+                - dot(g_got[rank:, :][:, block], z_sib[-1])
             )
             s_copy = send(s_next, got[height + 1][0], height + 1, 3 * height + 3)
             sends.append(s_copy)
@@ -220,39 +217,40 @@
             k_copy = send(k_next, got[height + 1][2], height + 1, 3 * height + 5)
             sends.append(k_copy)
             g_copy = advance_gram(height + 1, g_copy)
-    k_copy.wait_recv()
-    for copy in sends:
-        copy.wait_send()
-
     rows = levels * rank
     scale = 1.0 / math.sqrt(cols)
     z_all = jnp.concatenate(z_own, 0)
+    areas = [pl.ds(n * rows, rows) for n in range(3)]
     packed[:rank, :] = z_sib[0]
     packed[rank:rows, :] = z_all[rank:]
-    l_list = []
+    last = [send(packed.at[areas[0]], other.at[areas[0]], 0, 3 * levels)]
+    z_out[:, keep] = z_all
+    l_first = (s_ref[:rank, keep] - dot(g_ref[:rank, :], z_all)) * scale
+    packed[rows : rows + rank, :] = l_first
     for height in range(levels):
         shift = rank * height - rank * height // 128 * 128
+        part = slice(height * rank, (height + 1) * rank)
         chain = jnp.concatenate([z_sib[height]] + z_own[height + 1 :], 0)
         row = got[height][1][:rank, :][:, shift:]
-        l_list.append((got[height][0][:rank, :] - dot(row, chain, precision=HI)) * scale)
-    l_first = (s_ref[:rank, keep] - dot(g_ref[:rank, :], z_all, precision=HI)) * scale
-    packed[rows : rows + rank, :] = l_first
+        l_part = (got[height][0][:rank, :] - dot(row, chain)) * scale
+        l_out[part, keep] = l_part
+        if height > 0:
+            packed[rows + height * rank : rows + (height + 1) * rank, :] = l_part
+    last.append(send(packed.at[areas[1]], other.at[areas[1]], 0, 3 * levels + 1))
+    k_copy.wait_recv()
     packed[2 * rows : 2 * rows + rank, :] = k_ref[:rank, keep] * scale
-    z_out[:, keep] = z_all
     for height in range(levels):
         part = slice(height * rank, (height + 1) * rank)
         k_part = got[height][2][:rank, :] * scale
-        l_out[part, keep] = l_list[height]
         k_out[part, keep] = k_part
         if height > 0:
-            packed[rows + height * rank : rows + (height + 1) * rank, :] = l_list[height]
             packed[2 * rows + height * rank : 2 * rows + (height + 1) * rank, :] = k_part
-    last = send(packed, other, 0, 3 * levels)
-    last.wait_recv()
-    z_out[:, give] = other[:rows, :]
-    l_out[:, give] = other[rows : 2 * rows, :]
-    k_out[:, give] = other[2 * rows :, :]
-    last.wait_send()
+    last.append(send(packed.at[areas[2]], other.at[areas[2]], 0, 3 * levels + 2))
+    for copy, target, area in zip(last, (z_out, l_out, k_out), areas):
+        copy.wait_recv()
+        target[:, give] = other[area, :]
+    for copy in sends + last:
+        copy.wait_send()
 
 
 def tree_scratch(levels, rank, rows, cols, node_shape):
@@ -269,7 +267,7 @@
         got += group
         if height > 0:
             own += group
-    count = 3 * levels + 1
+    count = 3 * levels + 3
     return (
         [pltpu.VMEM((levels,) + node_shape, jnp.float32)]
         + own

time: 39.3 us -> 38.2 us (0.972)
  Pallas kernels: 37.8 us -> 36.8 us
    pallas_call x1, Pallas kernels: 30.9 us -> 29.8 us  [whole_tree(): pl.pallas_call(functools.partial(whole_kernel, levels, rank, tile), out_s...]
where the time goes in v4:
time: 38.2 us; the launch traced here: 38 us
  Pallas kernels  36.8 us (96%)
  between operations  1.29 us (3%)
    pallas_call x1, Pallas kernels, whole_tree(): pl.pallas_call(functools.partial(whole_kernel, levels, rank, tile), out_s...  29.8 us
    pallas_call x1, Pallas kernels, body(): pl.pallas_call(close_kernel, grid=grid, out_shape=[jax.ShapeDtypeStruct((...  6.95 us

profile of v4, /device:TPU:0, one launch (start us, length us, event | category | flops | bytes accessed | tf_op | source)
XLA Modules:
  0.0 38.0 jit_solution(7939033638804394646)
XLA Ops:
  1.3 29.8 %shard_map.85 = (f32[256,256]{1,0:T(8,128)}, f32[256,256]{1,0:T(8,128)}, f32[256,256]{1,0:T(8,128)}) custom-call(s32[1]{0:T(128)S(6)} %copy.9.rows_ref, f32[2048,256]{1,0:T(8,128)} %right_ref.3, f32[2048,256]{1,0:T(8,128)} %cot_ref.3, f32[256,2048]{1,0:T(8,128)} %bitcast.6, f32[256,2048]{1,0:T(8,128)} %bitcast.4, f32[15,128,128]{2,1,0:T(8,128)} %node_ref.1), custom_call_target="tpu_custom_call" | custom-call | tf_op jit(solution)/shard_map/pallas_call | solution.py:303
  31.1 7.0 %shard_map.86 = (f32[2048,256]{1,0:T(8,128)}, bf16[256,2048]{1,0:T(8,128)(2,1)}, bf16[256,2048]{1,0:T(8,128)(2,1)}) custom-call(s32[1]{0:T(128)S(6)} %copy.9.rows_ref, f32[2048,256]{1,0:T(8,128)} %right_ref.3, f32[2048,256]{1,0:T(8,128)} %cot_ref.3, f32[256,2048]{1,0:T(8,128)} %bitcast.5, f32[256,256]{1,0:T(8,128)} %get-tuple-element.9.z_ref, ...), custom_call_target="tpu_custom_call" | custom-call | tf_op jit(solution)/shard_map/pallas_call | solution.py:410

commit v5 on v4

--- a/solution.py
+++ b/solution.py
@@ -167,14 +167,26 @@
     k_all = [k_ref.at[:, keep]] + [own[n][2] for n in range(1, levels)]
     sends = []
 
+    def half_rows(height):
+        size = g_all[height].shape[0] // 2
+        return pl.ds(pl.multiple_of(mine * size, 8), size)
+
     def advance_gram(height, copy):
         copy.wait_recv()
+        if height == 1:
+            area = got[1][1].at[half_rows(1), :]
+            relay = send(area, area, 0, 3 * levels + 3)
+            sends.append(relay)
+            relay.wait_recv()
         if height == levels - 1:
             return None
         g_now, g_got, g_next = g_all[height], got[height][1], g_all[height + 1]
         skip = g_now.shape[1] - g_next.shape[1]
         g_next[...] = g_now[rank:, skip:] + g_got[rank:, skip:]
-        sends.append(send(g_next, got[height + 1][1], height + 1, 3 * height + 4))
+        source, target = g_next, got[height + 1][1]
+        if height == 0:
+            source, target = source.at[half_rows(1), :], target.at[half_rows(1), :]
+        sends.append(send(source, target, height + 1, 3 * height + 4))
         return sends[-1]
 
     g_copy = send(g_ref, got[0][1], 0, 1)
@@ -267,7 +279,7 @@
         got += group
         if height > 0:
             own += group
-    count = 3 * levels + 3
+    count = 3 * levels + 4
     return (
         [pltpu.VMEM((levels,) + node_shape, jnp.float32)]
         + own

time: 38.2 us -> 36.4 us (0.953)
  Pallas kernels: 36.8 us -> 34.9 us
    pallas_call x1, Pallas kernels: 29.8 us -> 27.9 us  [whole_tree(): pl.pallas_call(functools.partial(whole_kernel, levels, rank, tile), out_s...]
where the time goes in v5:
time: 36.4 us; the launch traced here: 36.2 us
  Pallas kernels  34.9 us (96%)
  between operations  1.29 us (4%)
    pallas_call x1, Pallas kernels, whole_tree(): pl.pallas_call(functools.partial(whole_kernel, levels, rank, tile), out_s...  27.9 us
    pallas_call x1, Pallas kernels, body(): pl.pallas_call(close_kernel, grid=grid, out_shape=[jax.ShapeDtypeStruct((...  6.95 us

profile of v5, /device:TPU:0, one launch (start us, length us, event | category | flops | bytes accessed | tf_op | source)
XLA Modules:
  0.0 36.2 jit_solution(1859313048855300439)
XLA Ops:
  1.3 27.9 %shard_map.85 = (f32[256,256]{1,0:T(8,128)}, f32[256,256]{1,0:T(8,128)}, f32[256,256]{1,0:T(8,128)}) custom-call(s32[1]{0:T(128)S(6)} %copy.9.rows_ref, f32[2048,256]{1,0:T(8,128)} %right_ref.3, f32[2048,256]{1,0:T(8,128)} %cot_ref.3, f32[256,2048]{1,0:T(8,128)} %bitcast.6, f32[256,2048]{1,0:T(8,128)} %bitcast.4, f32[15,128,128]{2,1,0:T(8,128)} %node_ref.1), custom_call_target="tpu_custom_call" | custom-call | tf_op jit(solution)/shard_map/pallas_call | solution.py:315
  29.2 6.9 %shard_map.86 = (f32[2048,256]{1,0:T(8,128)}, bf16[256,2048]{1,0:T(8,128)(2,1)}, bf16[256,2048]{1,0:T(8,128)(2,1)}) custom-call(s32[1]{0:T(128)S(6)} %copy.9.rows_ref, f32[2048,256]{1,0:T(8,128)} %right_ref.3, f32[2048,256]{1,0:T(8,128)} %cot_ref.3, f32[256,2048]{1,0:T(8,128)} %bitcast.5, f32[256,256]{1,0:T(8,128)} %get-tuple-element.9.z_ref, ...), custom_call_target="tpu_custom_call" | custom-call | tf_op jit(solution)/shard_map/pallas_call | solution.py:422

commit v6 on v5

--- a/solution.py
+++ b/solution.py
@@ -173,9 +173,9 @@
 
     def advance_gram(height, copy):
         copy.wait_recv()
-        if height == 1:
-            area = got[1][1].at[half_rows(1), :]
-            relay = send(area, area, 0, 3 * levels + 3)
+        if 0 < height < levels - 1:
+            area = got[height][1].at[half_rows(height), :]
+            relay = send(area, area, 0, 3 * levels + 2 + height)
             sends.append(relay)
             relay.wait_recv()
         if height == levels - 1:
@@ -184,8 +184,9 @@
         skip = g_now.shape[1] - g_next.shape[1]
         g_next[...] = g_now[rank:, skip:] + g_got[rank:, skip:]
         source, target = g_next, got[height + 1][1]
-        if height == 0:
-            source, target = source.at[half_rows(1), :], target.at[half_rows(1), :]
+        if height < levels - 2:
+            area = half_rows(height + 1)
+            source, target = source.at[area, :], target.at[area, :]
         sends.append(send(source, target, height + 1, 3 * height + 4))
         return sends[-1]
 
@@ -279,7 +280,7 @@
         got += group
         if height > 0:
             own += group
-    count = 3 * levels + 4
+    count = 4 * levels + 1
     return (
         [pltpu.VMEM((levels,) + node_shape, jnp.float32)]
         + own

time: 36.4 us -> 35.7 us (0.981)
  Pallas kernels: 34.9 us -> 34.3 us
    pallas_call x1, Pallas kernels: 27.9 us -> 27.3 us  [whole_tree(): pl.pallas_call(functools.partial(whole_kernel, levels, rank, tile), out_s...]
where the time goes in v6:
time: 35.7 us; the launch traced here: 35.5 us
  Pallas kernels  34.3 us (96%)
  between operations  1.29 us (4%)
    pallas_call x1, Pallas kernels, whole_tree(): pl.pallas_call(functools.partial(whole_kernel, levels, rank, tile), out_s...  27.3 us
    pallas_call x1, Pallas kernels, body(): pl.pallas_call(close_kernel, grid=grid, out_shape=[jax.ShapeDtypeStruct((...  6.95 us

profile of v6, /device:TPU:0, one launch (start us, length us, event | category | flops | bytes accessed | tf_op | source)
XLA Modules:
  0.0 35.5 jit_solution(17650580578445514300)
XLA Ops:
  1.3 27.3 %shard_map.85 = (f32[256,256]{1,0:T(8,128)}, f32[256,256]{1,0:T(8,128)}, f32[256,256]{1,0:T(8,128)}) custom-call(s32[1]{0:T(128)S(6)} %copy.9.rows_ref, f32[2048,256]{1,0:T(8,128)} %right_ref.3, f32[2048,256]{1,0:T(8,128)} %cot_ref.3, f32[256,2048]{1,0:T(8,128)} %bitcast.6, f32[256,2048]{1,0:T(8,128)} %bitcast.4, f32[15,128,128]{2,1,0:T(8,128)} %node_ref.1), custom_call_target="tpu_custom_call" | custom-call | tf_op jit(solution)/shard_map/pallas_call | solution.py:316
  28.6 7.0 %shard_map.86 = (f32[2048,256]{1,0:T(8,128)}, bf16[256,2048]{1,0:T(8,128)(2,1)}, bf16[256,2048]{1,0:T(8,128)(2,1)}) custom-call(s32[1]{0:T(128)S(6)} %copy.9.rows_ref, f32[2048,256]{1,0:T(8,128)} %right_ref.3, f32[2048,256]{1,0:T(8,128)} %cot_ref.3, f32[256,2048]{1,0:T(8,128)} %bitcast.5, f32[256,256]{1,0:T(8,128)} %get-tuple-element.9.z_ref, ...), custom_call_target="tpu_custom_call" | custom-call | tf_op jit(solution)/shard_map/pallas_call | solution.py:423
